TPU v7x, 512 devices: a whole 4x4x16 slice. The times are simulated.
512 devices in a mesh: pix: 128 (over z_hi, x, y, core), row: 4 (over z_lo).
Axes of the slice: x: 4, y: 4, z: 16 (z_hi: 4, z_lo: 4; z = z_hi * 4 + z_lo), core: 2. Of those that a mesh axis runs over, the one named last changes fastest.
Arguments:
- band_images: bfloat16 [256, 128, 8192], P('pix', 'row'), may hold values from -6 to 6
- pivots: int32 [2, 32], replicated, may hold values from 0 to 1048575, as said below
Outputs:
- residual: bfloat16 [8192, 128, 256], P(('pix', 'row'))
- coefficients: bfloat16 [64, 8192, 128], P(None, ('pix', 'row'))
Inputs may be any that keep to these rules, and one draw needn't show every extreme that they name: All 64 pivots lie in different columns, and every group of 32 lines starting at a multiple of 32 holds at least one pivot.
All inputs are finite; a program needn't handle non-finite values.
Results may differ from a plain program's by a relative error of at most 0.001.
Values may be sent and summed in bfloat16 or wider, within the bound.
A program may use at most 192 MiB of HBM per device.

v0:
```python
import jax
import jax.numpy as jnp
from jax import lax
from jax.sharding import PartitionSpec as P

highest = lax.Precision.HIGHEST


def orthonormal(spectra):
    gram = jnp.dot(spectra, spectra.T, precision=highest)
    factor = jnp.linalg.cholesky(gram)
    return jax.scipy.linalg.solve_triangular(factor, spectra, lower=True)


def project(block, basis):
    count = basis.shape[0] // 2
    first = basis[:count]
    second = basis[count:]
    coef_one = jnp.einsum("clb,kb->kcl", block, first, precision=highest)
    remain = block - jnp.einsum("kcl,kb->clb", coef_one, first, precision=highest)
    coef_two = jnp.einsum("clb,kb->kcl", remain, second, precision=highest)
    remain = remain - jnp.einsum("kcl,kb->clb", coef_two, second, precision=highest)
    return (
        remain.astype(jnp.bfloat16),
        jnp.concatenate([coef_one, coef_two], axis=0).astype(jnp.bfloat16),
    )


def shards(band_images, pivots):
    band_dev, line_dev, cols_all = band_images.shape
    pix_count = lax.axis_size("pix")
    row_count = lax.axis_size("row")
    narrow = cols_all // (pix_count * row_count)
    flat_pivots = pivots.reshape(-1)
    line_index = flat_pivots // cols_all
    column = flat_pivots % cols_all
    offset = line_index - lax.axis_index("row") * line_dev
    inside = (offset >= 0) & (offset < line_dev)
    position = jnp.clip(offset, 0, line_dev - 1) * cols_all + column
    picked = jnp.take(band_images.reshape(band_dev, line_dev * cols_all), position, axis=1)
    picked = jnp.where(inside[None, :], picked, jnp.zeros_like(picked))
    placed = jnp.zeros((band_dev * pix_count, flat_pivots.shape[0]), jnp.float32)
    placed = lax.dynamic_update_slice_in_dim(
        placed, picked.astype(jnp.float32), lax.axis_index("pix") * band_dev, 0
    )
    spectra = lax.psum(placed, ("pix", "row"))
    basis = orthonormal(spectra.T)
    shaped = band_images.reshape(band_dev, line_dev, pix_count, row_count, narrow)
    arrived = lax.all_to_all(
        lax.all_to_all(shaped, "pix", split_axis=2, concat_axis=0, tiled=True),
        "row",
        split_axis=3,
        concat_axis=1,
        tiled=True,
    )
    block = (
        arrived.reshape(arrived.shape[0], arrived.shape[1], narrow)
        .transpose(2, 1, 0)
        .astype(jnp.float32)
    )
    return project(block, basis)


def solution(mesh):
    placed = (P("pix", "row", None), P())
    return jax.shard_map(
        shards,
        mesh=mesh,
        in_specs=placed,
        out_specs=(P(("pix", "row"), None, None), P(None, ("pix", "row"), None)),
        check_vma=False,
    )
```

profile of v0, /device:TPU:1, one launch (start us, length us, event | category | flops | bytes accessed | tf_op | source)
XLA Modules:
  0.0 625.1 jit_solution(1769854623598273289)
XLA Ops:
  7.2 4.6 copy.14
  11.7 5.6 copy.22
  17.3 6.5 %reshape.198 = bf16[128,2,2048]{2,1,0:T(2,128)(2,1)S(1)} reshape(bf16[128,2,4,16,32]{4,3,2,1,0:T(8,128)(2,1)} %bitcast.50) | data formatting | bytes 2097152
  23.8 76.3 %all_to_all.33 = bf16[128,2,2048]{2,1,0:T(2,128)(2,1)S(1)} all-to-all(bf16[128,2,2048]{2,1,0:T(2,128)(2,1)S(1)} %reshape.198), channel_id=1, replica_groups=mesh['pix'=128,'row'=4] {'pix'}, dimensions={0} | all-to-all | bytes 2097152 | tf_op jit(solution)/shard_map/all_to_all | solution.py:50
  100.1 3.5 reshape.199
  103.6 6.9 %copy.16 = bf16[256,32,1,4,16]{0,4,2,1,3:T(8,128)(2,1)} copy(bf16[256,32,1,4,16]{1,4,3,0,2:T(8,128)(2,1)} %bitcast.49) | data formatting | bytes 2097152 | tf_op jit(solution)/shard_map/all_to_all | solution.py:50
  110.6 8.3 %all-to-all-start.1 = ((bf16[256,32,1,4,16]{0,4,2,1,3:T(8,128)(2,1)}), bf16[256,32,1,4,16]{0,4,2,1,3:T(8,128)(2,1)S(1)}, u32[]{:S(2)}, u32[]{:S(2)}) async-start(bf16[256,32,1,4,16]{0,4,2,1,3:T(8,128)(2,1)} %copy.16), calls=%async_computation.1 | async-start | bytes 2097152 | tf_op jit(solution)/shard_map/all_to_all | solution.py:49
  119.0 40.3 %copy.18 = bf16[2,32,8192]{0,2,1:T(8,128)(2,1)} copy(bf16[2,32,8192]{2,1,0:T(8,128)(2,1)S(1)} %copy-done) | data formatting | bytes 2097152 | tf_op args[0]
  159.4 1.5 gather_fusion
  161.0 0.6 dynamic_update_slice.3
  161.6 0.6 copy-done.1
  162.3 432.6 %all-reduce.2.cloned.1.call-done = f32[256,64]{0,1:T(8,128)} async-done(((f32[256,64]{0,1:T(8,128)}), f32[256,64]{0,1:T(8,128)}) %all-reduce.2.cloned.1.call-update) | async-done | bytes 65552 | tf_op jit(solution)/shard_map/psum | solution.py:46
  594.9 1.1 fusion.13
  596.1 5.8 cholesky.16
  602.0 0.6 compare_reduce_fusion
  602.7 0.7 fusion
  603.3 4.9 custom-call.7
  608.2 1.1 fusion.1
  609.3 0.3 copy.17
  609.7 1.0 fusion.12
  610.7 1.8 convert_subtract_fusion
  612.5 2.0 fusion.11
  614.6 0.9 copy.20
  615.5 2.8 subtract_convert_fusion
  (20 shorter events, 0.5 us)
Async XLA Ops:
  110.6 8.3 %copy-start.2 = (s32[2,32]{1,0:T(2,128)S(1)}, s32[2,32]{1,0:T(2,128)}, u32[]{:S(2)}) copy-start(s32[2,32]{1,0:T(2,128)} %param.3) | copy-start | bytes 772
  110.6 8.4 %copy-start = (bf16[2,32,8192]{2,1,0:T(8,128)(2,1)S(1)}, bf16[2,32,8192]{2,1,0:T(8,128)(2,1)}, u32[]{:S(2)}) copy-start(bf16[2,32,8192]{2,1,0:T(8,128)(2,1)} %param.2) | copy-start | bytes 3145732
  110.6 498.8 %all-to-all-start.1 = ((bf16[256,32,1,4,16]{0,4,2,1,3:T(8,128)(2,1)}), bf16[256,32,1,4,16]{0,4,2,1,3:T(8,128)(2,1)S(1)}, u32[]{:S(2)}, u32[]{:S(2)}) async-start(bf16[256,32,1,4,16]{0,4,2,1,3:T(8,128)(2,1)} %copy.16), calls=%async_computation.1 | async-start | bytes 2097152 | tf_op jit(solution)/shard_map/all_to_all | solution.py:49
  118.8 476.1 %all-reduce.2.cloned.1.call-start = ((), (), s32[]{:S(2)}) async-start(), calls=%async_computation.2 | async-start | bytes 131072 | tf_op jit(solution)/shard_map/psum | solution.py:46
  161.6 0.6 copy-start.1
Sparse Core Ops, SparseCore 0:
  162.4 432.4 all-reduce.1
where the time goes:
time: 626 us; the launch traced here: 625 us
  waiting for transfers between devices  433 us (69%)
  blocking collectives  76.3 us (12%)
  local copies, waits for them, and re-layouts  71.7 us (11%)
  between operations  14.2 us (2%)
  other arithmetic  12.2 us (2%)
  matrix products  9.87 us (2%)
  starting transfers between devices  8.26 us (1%)
    psum x1, waiting for transfers between devices, shards(): spectra = lax.psum(placed, ('pix', 'row'))  433 us
    all_to_all x1, blocking collectives, shards(): lax.all_to_all(shaped, 'pix', split_axis=2, concat_axis=0, tiled=True)  76.3 us
    unnamed x11, local copies, waits for them, and re-layouts  56.5 us
  transfers between devices with their start and end apart: 2, of which 1 were waited for; matrix products, arithmetic and copies ran while one was open for 9% of the time, Pallas kernels for 0%

commit v1 on v0

--- a/solution.py
+++ b/solution.py
@@ -2,6 +2,7 @@
 import jax.numpy as jnp
 from jax import lax
 from jax.sharding import PartitionSpec as P
+from jax.lax import all_gather
 
 highest = lax.Precision.HIGHEST
 
@@ -43,7 +44,7 @@
     placed = lax.dynamic_update_slice_in_dim(
         placed, picked.astype(jnp.float32), lax.axis_index("pix") * band_dev, 0
     )
-    spectra = lax.psum(placed, ("pix", "row"))
+    spectra = jnp.sum(all_gather(placed, ("pix", "row")), axis=0)
     basis = orthonormal(spectra.T)
     shaped = band_images.reshape(band_dev, line_dev, pix_count, row_count, narrow)
     arrived = lax.all_to_all(

time: 626 us -> 1610 us (2.57); the launches traced: 625 us -> 1580 us
  waiting for transfers between devices: 433 us -> 1350 us
  blocking collectives: 76.3 us -> 111 us
    all_gather x0 -> x1, waiting for transfers between devices: none -> 1350 us  [shards(): spectra = jnp.sum(all_gather(placed, ('pix', 'row')), axis=0)]
    psum x1 -> x0, waiting for transfers between devices: 433 us -> none  [shards(): spectra = lax.psum(placed, ('pix', 'row'))]
    all_to_all x0 -> x1, blocking collectives: none -> 35.3 us  [shards(): lax.all_to_all(lax.all_to_all(shaped, 'pix', split_axis=2, concat_axis=0,...]
    unnamed x11 -> x9, local copies, waits for them, and re-layouts: 56.5 us -> 56 us
  transfers between devices with their start and end apart: 2 -> 1, of which waited for: 1 -> 1; matrix products, arithmetic and copies ran while one was open for 9% -> 2% of each run, Pallas kernels for 0% -> 0%
where the time goes in v1:
time: 1610 us; the launch traced here: 1580 us
  waiting for transfers between devices  1350 us (84%)
  blocking collectives  111 us (7%)
  local copies, waits for them, and re-layouts  71.9 us (4%)
  other arithmetic  25.1 us (2%)
    all_gather x1, waiting for transfers between devices, shards(): spectra = jnp.sum(all_gather(placed, ('pix', 'row')), axis=0)  1350 us
    all_to_all x1, blocking collectives, shards(): lax.all_to_all(shaped, 'pix', split_axis=2, concat_axis=0, tiled=True)  76.1 us
    unnamed x9, local copies, waits for them, and re-layouts  56 us
    all_to_all x1, blocking collectives, shards(): lax.all_to_all(lax.all_to_all(shaped, 'pix', split_axis=2, concat_axis=0,...  35.3 us
  transfers between devices with their start and end apart: 1, of which 1 were waited for; matrix products, arithmetic and copies ran while one was open for 2% of the time, Pallas kernels for 0%

profile of v1, /device:TPU:1, one launch (start us, length us, event | category | flops | bytes accessed | tf_op | source)
XLA Modules:
  0.0 1581.2 jit_solution(17825714756841806432)
XLA Ops:
  7.2 0.8 reshape.241
  8.0 0.8 reshape.243
  8.8 41.2 %copy.29 = bf16[2,32,8192]{0,2,1:T(8,128)(2,1)} copy(bf16[2,32,8192]{2,1,0:T(8,128)(2,1)} %param.2) | data formatting | bytes 2097152 | tf_op args[0]
  50.1 1.5 gather_fusion
  51.8 0.6 dynamic_update_slice.4
  52.4 0.6 copy-done.1
  53.1 3.1 copy.25
  56.2 5.5 copy.35
  61.7 6.5 reshape.254
  68.3 76.1 %all_to_all.33 = bf16[128,2,2048]{2,1,0:T(2,128)(2,1)S(1)} all-to-all(bf16[128,2,2048]{2,1,0:T(2,128)(2,1)S(1)} %reshape.254), channel_id=1, replica_groups=mesh['pix'=128,'row'=4] {'pix'}, dimensions={0} | all-to-all | bytes 2097152 | tf_op jit(solution)/shard_map/all_to_all | solution.py:51
  144.4 3.5 reshape.255
  147.9 6.1 copy.27
  154.1 35.3 %all_to_all.34 = bf16[256,32,1,4,16]{0,4,2,1,3:T(8,128)(2,1)S(1)} all-to-all(bf16[256,32,1,4,16]{0,4,2,1,3:T(8,128)(2,1)S(1)} %copy.27), channel_id=1, replica_groups=mesh['pix'=128,'row'=4] {'row'}, dimensions={3} | all-to-all | bytes 2097152 | tf_op jit(solution)/shard_map/all_to_all | solution.py:50
  189.8 1350.5 %all-gather.2.cloned.1.call-done = f32[512,256,64]{1,2,0:T(8,128)} async-done(((f32[1,256,64]{1,2,0:T(8,128)}), f32[512,256,64]{1,2,0:T(8,128)}) %all-gather.2.cloned.1.call-update) | async-done | bytes 33554448 | tf_op jit(solution)/shard_map/all_gather | solution.py:47
  1540.2 12.9 reduce_sum.9
  1553.5 5.8 cholesky.16
  1559.3 0.6 compare_reduce_fusion
  1560.0 0.7 fusion
  1560.6 4.9 custom-call.7
  1565.8 1.0 fusion.13
  1566.8 1.8 convert_subtract_fusion
  1568.7 2.0 fusion.12
  1570.7 0.9 copy.33
  1571.6 2.8 subtract_convert_fusion
  (20 shorter events, 1.3 us)
Async XLA Ops:
  7.2 1533.1 %all-gather.2.cloned.1.call-start = ((), (), s32[]{:S(2)}) async-start(), calls=%async_computation.2 | async-start | bytes 33619968 | tf_op jit(solution)/shard_map/all_gather | solution.py:47
  8.8 44.2 %copy-start = (bf16[2,32,8192]{2,1,0:T(8,128)(2,1)S(1)}, bf16[2,32,8192]{2,1,0:T(8,128)(2,1)}, u32[]{:S(2)}) copy-start(bf16[2,32,8192]{2,1,0:T(8,128)(2,1)} %param.2) | copy-start | bytes 3145732
  52.4 0.6 copy-start.1
Sparse Core Ops, SparseCore 0:
  53.2 1487.0 all-gather.1
